TPU v7x, 32 devices: a whole 2x2x4 slice. The times are simulated.
32 devices in a mesh: mode: 8 (over z, x), var: 4 (over y, core).
Axes of the slice: x: 2, y: 2, z: 4, core: 2. Of those that a mesh axis runs over, the one named last changes fastest.
Arguments:
- control: bfloat16 [1, 4, 8, 1024, 1024], P(None, 'var', 'mode'), may hold values from -6 to 6
- filters: bfloat16 [3, 1024, 1024], replicated, may hold values from -4 to 5
- weights: bfloat16 [4, 3, 1024, 1024], P('var'), may hold values from 0.29882812 to 3
- vertical: bfloat16 [4, 64, 8], replicated, may hold values from -2 to 2
- balance: bfloat16 [3, 64, 64], replicated, may hold values from -0.75 to 0.75
Outputs:
- increment: bfloat16 [1, 4, 64, 1024, 1024], P(None, 'var', 'mode')
All inputs are finite; a program needn't handle non-finite values.
Results may differ from a plain program's by a relative error of at most 0.006.
Values may be sent and summed in bfloat16 or wider, within the bound.
A program may use at most 128 MiB of HBM per device.

v0:
```python
import jax
import jax.numpy as jnp
from jax import lax
from jax.sharding import PartitionSpec as P


def smooth(planes, filters, weights):
    total = jnp.zeros(planes.shape, jnp.float32)
    for k in range(filters.shape[0]):
        half = jnp.einsum(
            "ij,pjc->pic", filters[k], planes, preferred_element_type=jnp.float32
        ).astype(jnp.bfloat16)
        full = jnp.einsum("pic,dc->pid", half, filters[k], preferred_element_type=jnp.float32)
        total = total + weights[k].astype(jnp.float32) * full
    return total.astype(jnp.bfloat16)


def per_device(control, filters, weights, vertical, balance):
    members, _, depth, rows, cols = control.shape
    nmode = lax.axis_size("mode")
    nvar = lax.axis_size("var")
    strip = rows // (nmode * nvar)
    levcount = vertical.shape[1]
    filtered = smooth(control.reshape(members * depth, rows, cols), filters, weights[0])
    filtered = filtered.reshape(members, 1, depth, nvar, nmode, strip, cols)
    blocks = lax.all_to_all(
        lax.all_to_all(filtered, "mode", split_axis=4, concat_axis=2, tiled=True),
        "var",
        split_axis=3,
        concat_axis=1,
        tiled=True,
    )
    modecount = blocks.shape[2]
    blocks = blocks.reshape(members, nvar, modecount, strip * cols)
    levels = jnp.einsum("vlq,mvqc->mvlc", vertical, blocks, preferred_element_type=jnp.float32)
    stream = levels[:, 0].astype(jnp.bfloat16)
    extra = jnp.einsum("vlk,mkc->mvlc", balance, stream, preferred_element_type=jnp.float32)
    result = jnp.concatenate([levels[:, :1], levels[:, 1:] + extra], axis=1).astype(jnp.bfloat16)
    result = result.reshape(members, nvar, levcount, 1, 1, strip, cols)
    back = lax.all_to_all(
        lax.all_to_all(result, "mode", split_axis=2, concat_axis=4, tiled=True),
        "var",
        split_axis=1,
        concat_axis=3,
        tiled=True,
    )
    return back.reshape(members, 1, levcount // nmode, rows, cols)


def solution(mesh):
    in_specs = (P(None, "var", "mode", None, None), P(), P("var", None, None, None), P(), P())
    out_specs = P(None, "var", "mode", None, None)
    return jax.shard_map(
        per_device, mesh=mesh, in_specs=in_specs, out_specs=out_specs, check_vma=False
    )
```

profile of v0, /device:TPU:29, one launch (start us, length us, event | category | flops | bytes accessed | tf_op | source)
XLA Modules:
  0.0 737.2 jit_solution(12467179116577324104)
XLA Ops:
  0.0 0.0 copy-start
  0.0 1.6 copy-done
  1.6 8.9 %fusion.7 = f32[1024,1024]{1,0:T(8,128)} fusion(bf16[3,1024,1024]{2,1,0:T(8,128)(2,1)} %param.6, bf16[1,1,1,1024,1024]{4,3,2,1,0:T(8,128)(2,1)S(1)} %copy-done), kind=kOutput, calls=%fused_computation.15 | convolution fusion | flops 4296015872 | bytes 10485760 | tf_op jit(solution)/shard_map/pic,dc->pid/dot_general | solution.py:13
  10.5 8.7 %fusion.9 = f32[1024,1024]{1,0:T(8,128)} fusion(bf16[3,1024,1024]{2,1,0:T(8,128)(2,1)} %param.6, bf16[1,1,1,1024,1024]{4,3,2,1,0:T(8,128)(2,1)S(1)} %copy-done), kind=kOutput, calls=%fused_computation.17 | convolution fusion | flops 4296015872 | bytes 10485760 | tf_op jit(solution)/shard_map/pic,dc->pid/dot_general | solution.py:13
  19.2 12.5 %fusion.4 = bf16[1024,1024]{1,0:T(8,128)(2,1)} fusion(f32[1024,1024]{1,0:T(8,128)} %fusion.7, f32[1024,1024]{1,0:T(8,128)} %fusion.9, bf16[1,3,1024,1024]{3,2,1,0:T(8,128)(2,1)} %param.7, bf16[3,1024,1024]{2,1,0:T(8,128)(2,1)} %param.6, bf16[1,1,1,1024,1024]{4,3,2,1,0:T(8,128)(2,1)S(1)} %copy-done), kind=kOutput, calls=%fused_computation.10 | convolution fusion | flops 4305453056 | bytes 23068672 | tf_op jit(solution)/shard_map/pic,dc->pid/dot_general | solution.py:13
  31.7 1.8 copy.13
  33.5 51.0 %all_to_all.66 = bf16[1,1,1,4,8,32,1024]{6,5,3,2,1,0,4:T(8,128)(2,1)S(1)} all-to-all(bf16[1,1,1,4,8,32,1024]{6,5,3,2,1,0,4:T(8,128)(2,1)S(1)} %copy.13), channel_id=1, replica_groups=mesh['mode'=8,'var'=4] {'mode'}, dimensions={4} | all-to-all | bytes 4194304 | tf_op jit(solution)/shard_map/all_to_all | solution.py:27
  84.4 0.2 copy.14
  84.6 0.0 copy-start.4
  84.6 28.3 %all_to_all.67 = bf16[1,1,8,4,1,32,1024]{6,5,2,4,1,0,3:T(8,128)(2,1)} all-to-all(bf16[1,1,8,4,1,32,1024]{6,5,2,4,1,0,3:T(8,128)(2,1)S(1)} %copy.14), channel_id=1, replica_groups=mesh['mode'=8,'var'=4] {'var'}, dimensions={3} | all-to-all | bytes 4194304 | tf_op jit(solution)/shard_map/all_to_all | solution.py:26
  112.9 2.9 reshape.113
  115.8 0.0 copy-done.4
  115.8 13.1 %convolution_bitcast_fusion = f32[1,4,64,32768]{3,2,1,0:T(8,128)} fusion(bf16[4,8,32768]{2,1,0:T(8,128)(2,1)S(1)} %reshape.113, bf16[4,64,8]{1,2,0:T(8,128)(2,1)S(1)} %copy-done.4), kind=kOutput, calls=%fused_computation | convolution fusion | flops 134217728 | bytes 35655680 | tf_op jit(solution)/shard_map/vlq,mvqc->mvlc/dot_general | solution.py:35
  128.9 0.0 copy-start.3
  128.9 5.9 slice.82
  134.7 0.0 copy-done.3
  134.7 17.0 %fusion.1 = bf16[1,3,64,32768]{3,2,1,0:T(8,128)(2,1)} fusion(bf16[3,64,64]{2,1,0:T(8,128)(2,1)S(1)} %copy-done.3, f32[1,4,64,32768]{3,2,1,0:T(8,128)} %convolution_bitcast_fusion), kind=kOutput, calls=%fused_computation.3 | convolution fusion | flops 817889280 | bytes 41967616 | tf_op jit(solution)/shard_map/vlk,mkc->mvlc/dot_general | solution.py:37
  151.8 0.0 copy-start.2
  151.8 14.7 %copy.20 = bf16[24,8,32,1024]{3,2,1,0:T(8,128)(2,1)} copy(bf16[24,8,32,1024]{3,1,2,0:T(8,128)(2,1)} %bitcast.136) | data formatting | bytes 25165824
  166.4 0.0 copy-done.2
  166.4 2.5 copy.19
  168.9 7.2 pad_maximum_fusion
  176.1 365.8 %all_to_all.68 = bf16[1,4,64,1,1,32,1024]{6,5,1,4,3,0,2:T(8,128)(2,1)S(1)} all-to-all(bf16[1,4,64,1,1,32,1024]{6,5,1,4,3,0,2:T(8,128)(2,1)S(1)} %pad_maximum_fusion), channel_id=1, replica_groups=mesh['mode'=8,'var'=4] {'mode'}, dimensions={2} | all-to-all | bytes 33554432 | tf_op jit(solution)/shard_map/all_to_all | solution.py:41
  541.9 2.5 copy.24
  544.4 186.1 %all_to_all.69 = bf16[1,4,8,1,8,32,1024]{6,5,4,2,3,0,1:T(8,128)(2,1)S(1)} all-to-all(bf16[1,4,8,1,8,32,1024]{6,5,4,2,3,0,1:T(8,128)(2,1)S(1)} %bitcast.135), channel_id=1, replica_groups=mesh['mode'=8,'var'=4] {'var'}, dimensions={1} | all-to-all | bytes 33554432 | tf_op jit(solution)/shard_map/all_to_all | solution.py:40
  730.5 0.0 copy-start.1
  730.5 6.7 copy.18
  737.2 0.0 copy-done.1
Async XLA Ops:
  0.0 1.6 copy-start
  84.6 31.1 %copy-start.4 = (bf16[4,64,8]{1,2,0:T(8,128)(2,1)S(1)}, bf16[4,64,8]{1,2,0:T(8,128)(2,1)}, u32[]{:S(2)}) copy-start(bf16[4,64,8]{1,2,0:T(8,128)(2,1)} %param.8) | copy-start | bytes 12292
  128.9 5.9 copy-start.3
  151.8 14.7 %copy-start.2 = (bf16[1,1,64,32768]{3,2,1,0:T(8,128)(2,1)S(1)}, bf16[1,1,64,32768]{3,2,1,0:T(8,128)(2,1)}, u32[]{:S(2)}) copy-start(bf16[1,1,64,32768]{3,2,1,0:T(8,128)(2,1)} %slice.82) | copy-start | bytes 12582916
  730.5 6.7 copy-start.1
where the time goes:
time: 744 us; the launch traced here: 737 us
  blocking collectives  631 us (85%)
  matrix products  60.3 us (8%)
  local copies, waits for them, and re-layouts  38.5 us (5%)
    all_to_all x1, blocking collectives, per_device(): lax.all_to_all(result, 'mode', split_axis=2, concat_axis=4, tiled=True)  366 us
    all_to_all x1, blocking collectives, per_device(): lax.all_to_all(lax.all_to_all(result, 'mode', split_axis=2, concat_axis=4...  186 us
    all_to_all x1, blocking collectives, per_device(): lax.all_to_all(filtered, 'mode', split_axis=4, concat_axis=2, tiled=True)  51 us
    dot_general x3, matrix products, smooth(): jnp.einsum('pic,dc->pid', half, filters[k], preferred_element_type=jnp.fl...  30.1 us
    all_to_all x1, blocking collectives, per_device(): lax.all_to_all(lax.all_to_all(filtered, 'mode', split_axis=4, concat_axis...  28.3 us
    unnamed x12, local copies, waits for them, and re-layouts  18.8 us
    dot_general x1, matrix products, per_device(): jnp.einsum('vlk,mkc->mvlc', balance, stream, preferred_element_type=jnp.f...  17 us

commit v1 on v0

--- a/solution.py
+++ b/solution.py
@@ -15,7 +15,7 @@
     return total.astype(jnp.bfloat16)
 
 
-def per_device(control, filters, weights, vertical, balance):
+def per_device_exchange(control, filters, weights, vertical, balance):
     members, _, depth, rows, cols = control.shape
     nmode = lax.axis_size("mode")
     nvar = lax.axis_size("var")
@@ -47,9 +47,50 @@
     return back.reshape(members, 1, levcount // nmode, rows, cols)
 
 
+def coefficients(vertical, balance, var, mode, nmode):
+    nvar, levcount, _ = vertical.shape
+    mine = levcount // nmode
+    own = lax.dynamic_slice_in_dim(
+        lax.dynamic_index_in_dim(vertical, var, 0, keepdims=False), mode * mine, mine, 0
+    )
+    regress = lax.dynamic_slice_in_dim(
+        lax.dynamic_index_in_dim(balance, jnp.maximum(var - 1, 0), 0, keepdims=False),
+        mode * mine, mine, 0,
+    )
+    folded = jnp.dot(
+        regress.astype(jnp.float32), vertical[0].astype(jnp.float32), precision="highest"
+    )
+    folded = jnp.where(var > 0, folded, 0.0)
+    high = folded.astype(jnp.bfloat16)
+    low = (folded - high.astype(jnp.float32)).astype(jnp.bfloat16)
+    return own, high, low
+
+
+def per_device_gather(control, filters, weights, vertical, balance):
+    members, _, depth, rows, cols = control.shape
+    nmode = lax.axis_size("mode")
+    var = lax.axis_index("var")
+    filtered = smooth(control.reshape(members * depth, rows, cols), filters, weights[0])
+    first = lax.psum(jnp.where(var == 0, filtered, jnp.zeros_like(filtered)), "var")
+    both = jnp.stack([filtered, first]).reshape(2, members, depth, rows, cols)
+    both = lax.all_gather(both, "mode", axis=2, tiled=True)
+    own, high, low = coefficients(vertical, balance, var, lax.axis_index("mode"), nmode)
+    coef = jnp.stack([own, high], axis=1)
+    levels = jnp.einsum("lsq,smqrc->mlrc", coef, both, preferred_element_type=jnp.float32)
+    levels += jnp.einsum("lq,mqrc->mlrc", low, both[1], preferred_element_type=jnp.float32)
+    return levels.astype(jnp.bfloat16)[:, None]
+
+
 def solution(mesh):
     in_specs = (P(None, "var", "mode", None, None), P(), P("var", None, None, None), P(), P())
     out_specs = P(None, "var", "mode", None, None)
-    return jax.shard_map(
-        per_device, mesh=mesh, in_specs=in_specs, out_specs=out_specs, check_vma=False
-    )
+
+    def run(control, filters, weights, vertical, balance):
+        members, _, modes, rows, cols = control.shape
+        gather = modes * mesh.shape["mode"] <= vertical.shape[1] * 2
+        body = per_device_gather if gather else per_device_exchange
+        return jax.shard_map(
+            body, mesh=mesh, in_specs=in_specs, out_specs=out_specs, check_vma=False
+        )(control, filters, weights, vertical, balance)
+
+    return run

time: 744 us -> 835 us (1.12)
  waiting for transfers between devices: 0 us -> 689 us
  blocking collectives: 631 us -> 0 us
  matrix products: 60.3 us -> 88.9 us
  between operations: 0.06 us -> 13.4 us
    all_gather x0 -> x1, waiting for transfers between devices: none -> 637 us  [per_device_gather(): both = lax.all_gather(both, 'mode', axis=2, tiled=True)]
    all_to_all x4 -> x0, blocking collectives: 631 us -> none  [the longest x1 366 us: per_device(): lax.all_to_all(result, 'mode', split_axis=2, concat_axis=4, tiled=True)]
    psum x0 -> x1, waiting for transfers between devices: none -> 52.1 us  [per_device_gather(): lax.psum(jnp.where(var == 0, filtered, jnp.zeros_like(filtered)), 'var')]
    dot_general x2 -> x3, matrix products: 30.1 us -> 58.8 us  [the longest x1 33.1 us: per_device_gather(): jnp.einsum('lsq,smqrc->mlrc', coef, both, preferred_element_type=jnp.floa...]
    broadcast_in_dim x0 -> x1, local copies, waits for them, and re-layouts: none -> 18.8 us  [per_device_gather(): return levels.astype(jnp.bfloat16)[:, None]]
    unnamed x12 -> x9, local copies, waits for them, and re-layouts: 18.8 us -> 2.34 us
    another operation x1, local copies, waits for them, and re-layouts: 2.87 us -> 13.9 us  [run(): jax.shard_map(body, mesh=mesh, in_specs=in_specs, out_specs=out_specs, ch...]
    all_to_all x3 -> x0, local copies, waits for them, and re-layouts: 9.3 us -> none  [the longest x1 6.66 us: per_device(): lax.all_to_all(lax.all_to_all(result, 'mode', split_axis=2, concat_axis=4...]
  transfers between devices with their start and end apart: 0 -> 2, of which waited for: 0 -> 2; matrix products, arithmetic and copies ran while one was open for 0% -> 0% of each run, Pallas kernels for 0% -> 0%
where the time goes in v1:
time: 835 us; the launch traced here: 833 us
  waiting for transfers between devices  689 us (83%)
  matrix products  88.9 us (11%)
  local copies, waits for them, and re-layouts  35.1 us (4%)
  between operations  13.4 us (2%)
    all_gather x1, waiting for transfers between devices, per_device_gather(): both = lax.all_gather(both, 'mode', axis=2, tiled=True)  637 us
    psum x1, waiting for transfers between devices, per_device_gather(): lax.psum(jnp.where(var == 0, filtered, jnp.zeros_like(filtered)), 'var')  52.1 us
    dot_general x1, matrix products, per_device_gather(): jnp.einsum('lsq,smqrc->mlrc', coef, both, preferred_element_type=jnp.floa...  33.1 us
    dot_general x3, matrix products, smooth(): jnp.einsum('pic,dc->pid', half, filters[k], preferred_element_type=jnp.fl...  30.1 us
    dot_general x1, matrix products, per_device_gather(): jnp.einsum('lq,mqrc->mlrc', low, both[1], preferred_element_type=jnp.floa...  24.9 us
    broadcast_in_dim x1, local copies, waits for them, and re-layouts, per_device_gather(): return levels.astype(jnp.bfloat16)[:, None]  18.8 us
  transfers between devices with their start and end apart: 2, of which 2 were waited for; matrix products, arithmetic and copies ran while one was open for 0% of the time, Pallas kernels for 0%

profile of v1, /device:TPU:29, one launch (start us, length us, event | category | flops | bytes accessed | tf_op | source)
XLA Modules:
  0.0 832.6 jit_solution(7620966131374924242)
XLA Ops:
  6.5 0.0 copy-start
  6.5 0.0 all-reduce.2.cloned.1.call-start
  6.5 1.6 copy-done
  8.1 8.8 %fusion.12 = f32[1024,1024]{1,0:T(8,128)} fusion(bf16[3,1024,1024]{2,1,0:T(8,128)(2,1)} %param.6, bf16[1,1,1,1024,1024]{4,3,2,1,0:T(8,128)(2,1)S(1)} %copy-done), kind=kOutput, calls=%fused_computation.16 | convolution fusion | flops 4296015872 | bytes 10485760 | tf_op jit(solution)/shard_map/pic,dc->pid/dot_general | solution.py:13
  16.9 8.7 %fusion.14 = f32[1024,1024]{1,0:T(8,128)} fusion(bf16[3,1024,1024]{2,1,0:T(8,128)(2,1)} %param.6, bf16[1,1,1,1024,1024]{4,3,2,1,0:T(8,128)(2,1)S(1)} %copy-done), kind=kOutput, calls=%fused_computation.18 | convolution fusion | flops 4296015872 | bytes 10485760 | tf_op jit(solution)/shard_map/pic,dc->pid/dot_general | solution.py:13
  25.6 12.6 %fusion.9 = bf16[1024,1024]{1,0:T(8,128)(2,1)} fusion(f32[1024,1024]{1,0:T(8,128)} %fusion.12, f32[1024,1024]{1,0:T(8,128)} %fusion.14, bf16[1,3,1024,1024]{3,2,1,0:T(8,128)(2,1)} %param.7, bf16[3,1024,1024]{2,1,0:T(8,128)(2,1)} %param.6, bf16[1,1,1,1024,1024]{4,3,2,1,0:T(8,128)(2,1)S(1)} %copy-done), kind=kOutput, calls=%fused_computation.11 | convolution fusion | flops 4305453056 | bytes 23068672 | tf_op jit(solution)/shard_map/pic,dc->pid/dot_general | solution.py:13
  38.3 0.0 copy-start.2
  38.3 1.5 select_bitcast_fusion
  39.7 0.0 all-reduce.2.cloned.1.call-update
  39.7 0.2 all-gather.3.cloned.1.call-start
  40.0 52.1 %all-reduce.2.cloned.1.call-done = bf16[1,1,1024,1024]{3,2,1,0:T(8,128)(2,1)} async-done(((bf16[1,1,1024,1024]{3,2,1,0:T(8,128)(2,1)}), bf16[1,1,1024,1024]{3,2,1,0:T(8,128)(2,1)}) %all-reduce.2.cloned.1.call-update) | async-done | bytes 2097168 | tf_op jit(solution)/shard_map/psum | solution.py:74
  92.1 0.0 copy-done.2
  92.1 4.0 pad_maximum_fusion
  96.1 0.0 copy-start.3
  96.1 0.0 all-gather.3.cloned.1.call-update
  96.1 0.7 copy-done.3
  96.8 0.1 constant_dynamic-slice_fusion
  96.8 0.1 copy.11
  96.9 0.8 convolution_select_fusion
  97.7 637.3 %all-gather.3.cloned.1.call-done = bf16[2,8,1024,1024]{3,2,1,0:T(8,128)(2,1)} async-done(((bf16[2,1,1024,1024]{3,2,1,0:T(8,128)(2,1)}), bf16[2,8,1024,1024]{3,2,1,0:T(8,128)(2,1)}) %all-gather.3.cloned.1.call-update) | async-done | bytes 33554448 | tf_op jit(solution)/shard_map/all_gather | solution.py:76
  735.0 13.9 %slice_bitcast_fusion = bf16[8,1024,1024]{2,1,0:T(8,128)(2,1)} fusion(bf16[2,8,1024,1024]{3,2,1,0:T(8,128)(2,1)} %all-gather.3.cloned.1.call-done), kind=kLoop, calls=%fused_computation.5 | loop fusion | bytes 33554432 | tf_op jit(solution)/shard_map/reshape.25 | solution.py:92
  748.9 33.1 %fusion.1 = f32[1024,1024,8,1]{1,2,3,0:T(8,128)} fusion(bf16[2,8,1024,1024]{3,2,1,0:T(8,128)(2,1)} %all-gather.3.cloned.1.call-done, bf16[8,1,8]{2,0,1:T(8,128)(2,1)S(1)} %convert_bitcast_fusion, bf16[8,1,8]{2,0,1:T(8,128)(2,1)S(1)} %bitcast.110), kind=kOutput, calls=%fused_computation.2 | convolution fusion | flops 268435584 | bytes 67109120 | tf_op jit(solution)/shard_map/lsq,smqrc->mlrc/dot_general | solution.py:79
  782.1 24.9 %fusion.3 = bf16[1,1,8,1024,1024]{4,2,3,1,0:T(8,128)(2,1)} fusion(f32[1024,1024,8,1]{1,2,3,0:T(8,128)} %fusion.1, bf16[8,1024,1024]{2,1,0:T(8,128)(2,1)} %slice_bitcast_fusion, f32[8,8]{1,0:T(8,128)S(1)} %convolution_select_fusion), kind=kOutput, calls=%fused_computation.4 | convolution fusion | flops 150995200 | bytes 67109120 | tf_op jit(solution)/shard_map/lq,mqrc->mlrc/dot_general | solution.py:80
  807.0 0.0 copy-start.1
  807.0 18.8 %copy.9 = bf16[1,1,8,1024,1024]{4,3,2,1,0:T(8,128)(2,1)} copy(bf16[1,1,8,1024,1024]{4,2,3,1,0:T(8,128)(2,1)} %fusion.3) | data formatting | bytes 33554432 | tf_op jit(solution)/shard_map/broadcast_in_dim | solution.py:81
  825.8 0.0 copy-done.1
  (1 shorter events, 0.0 us)
Async XLA Ops:
  6.5 1.6 copy-start
  6.5 85.5 %all-reduce.2.cloned.1.call-start = ((), (), s32[]{:S(2)}) async-start(), calls=%async_computation | async-start | bytes 4194304 | tf_op jit(solution)/shard_map/psum | solution.py:74
  38.3 53.8 %copy-start.2 = (bf16[1024,1024]{1,0:T(8,128)(2,1)S(1)}, bf16[1024,1024]{1,0:T(8,128)(2,1)}, u32[]{:S(2)}) copy-start(bf16[1024,1024]{1,0:T(8,128)(2,1)} %fusion.9) | copy-start | bytes 6291460
  39.7 695.3 %all-gather.3.cloned.1.call-start = ((), (), s32[]{:S(2)}) async-start(), calls=%async_computation.1 | async-start | bytes 37748736 | tf_op jit(solution)/shard_map/all_gather | solution.py:76
  96.1 0.7 copy-start.3
  807.0 18.8 %copy-start.1 = (bf16[1,1,1,1024,1024]{4,3,2,1,0:T(8,128)(2,1)S(1)}, bf16[1,1,1,1024,1024]{4,3,2,1,0:T(8,128)(2,1)}, u32[]{:S(2)}) copy-start(bf16[1,1,1,1024,1024]{4,3,2,1,0:T(8,128)(2,1)} %param.5) | copy-start | bytes 6291460
Sparse Core Ops, SparseCore 0:
  39.9 52.1 all-reduce.1
  96.2 638.7 all-gather.2

commit v2 on v1

--- a/solution.py
+++ b/solution.py
@@ -1,6 +1,10 @@
+import functools
+
 import jax
 import jax.numpy as jnp
 from jax import lax
+from jax.experimental import pallas as pl
+from jax.experimental.pallas import tpu as pltpu
 from jax.sharding import PartitionSpec as P
 
 
@@ -66,28 +70,242 @@
     return own, high, low
 
 
+GROUP = 16
+LINE = 2
+
+
+def gather_kernel(
+    nmode, nvar, chunks, control, filters, weights, coef, out,
+    buf, stage, recv, line_send, tree_send, out_sem,
+):
+    mode, var = lax.axis_index("mode"), lax.axis_index("var")
+    z, x = mode // LINE, mode % LINE
+    nz = nmode // LINE
+    rows, cols = control.shape
+    strip = rows // chunks
+    own_lead = nz
+    tree_lead = nz + 2
+
+    even = var % 2 == 0
+    peers = [
+        (z < nz - 1, (mode + LINE, var)),
+        (z > 0, (mode - LINE, var)),
+        (var >= 0, (z * LINE + 1 - x, var)),
+    ]
+    first = var == 0
+    tree = [(even, (mode, var + 1))] + [
+        (first, (mode, jnp.int32(v))) for v in range(2, nvar, 2)
+    ]
+
+    barrier = pltpu.get_barrier_semaphore()
+    count = jnp.int32(0)
+    greet = peers + tree + [
+        (jnp.logical_not(even), (mode, var - 1)),
+        (jnp.logical_and(even, var > 0), (mode, jnp.int32(0))),
+    ]
+    for exists, device in greet:
+        @pl.when(exists)
+        def _(device=device):
+            pl.semaphore_signal(
+                barrier, inc=1, device_id=device, device_id_type=pl.DeviceIdType.MESH
+            )
+        count += exists.astype(jnp.int32)
+    pl.semaphore_wait(barrier, count)
+
+    def part(slot, j):
+        return buf.at[slot, pl.ds(pl.multiple_of(j * strip, strip), strip)]
+
+    def line_copy(way, slot, j):
+        return pltpu.make_async_remote_copy(
+            part(slot, j), part(slot, j), line_send.at[way, slot // LINE, j], recv.at[slot, j],
+            device_id=peers[way][1], device_id_type=pl.DeviceIdType.MESH,
+        )
+
+    def tree_copy(way, q, j):
+        source = jnp.where(first, q, q + nmode)
+        return pltpu.make_async_remote_copy(
+            part(source, j), part(q + nmode, j), tree_send.at[way, q, j], recv.at[q + nmode, j],
+            device_id=tree[way][1], device_id_type=pl.DeviceIdType.MESH,
+        )
+
+    def await_part(slot, j):
+        pltpu.make_async_copy(part(slot, j), part(slot, j), recv.at[slot, j]).wait()
+
+    def send_line(ways, slot, j):
+        for way in ways:
+            @pl.when(peers[way][0])
+            def _(way=way):
+                line_copy(way, slot, j).start()
+
+    def send_tree(q, j):
+        for way in range(len(tree)):
+            @pl.when(tree[way][0])
+            def _(way=way):
+                tree_copy(way, q, j).start()
+
+    def compute(j):
+        at = pl.ds(pl.multiple_of(j * strip, strip), strip)
+        total = jnp.zeros((strip, cols), jnp.float32)
+        for k in range(filters.shape[0]):
+            half = jnp.dot(filters[k, at], control[...], preferred_element_type=jnp.float32)
+            full = lax.dot_general(
+                half.astype(jnp.bfloat16), filters[k], (((1,), (1,)), ((), ())),
+                preferred_element_type=jnp.float32,
+            )
+            total += weights[k, at].astype(jnp.float32) * full
+        buf[mode, at] = total.astype(jnp.bfloat16)
+
+    levels = out.shape[0]
+
+    def out_copy(j):
+        at = pl.ds(pl.multiple_of(j * strip, strip), strip)
+        return pltpu.make_async_copy(stage.at[j % 2], out.at[:, at], out_sem.at[j % 2])
+
+    def combine(j):
+        @pl.when(j >= 2)
+        def _():
+            out_copy(j - 2).wait()
+
+        height = levels * GROUP
+
+        def put(i, sums):
+            stage[j % 2, :, pl.ds(pl.multiple_of(i * GROUP, GROUP), GROUP)] = sums.reshape(
+                levels, GROUP, cols
+            ).astype(jnp.bfloat16)
+
+        def group(i):
+            return pl.ds(pl.multiple_of(j * strip + i * GROUP, GROUP), GROUP)
+
+        @pl.when(first)
+        def _():
+            @pl.loop(0, strip // GROUP)
+            def _(i):
+                planes = buf[:nmode, group(i)].reshape(nmode * GROUP, cols)
+                put(i, jnp.dot(
+                    coef[:height, : nmode * GROUP], planes, preferred_element_type=jnp.float32
+                ))
+
+        @pl.when(jnp.logical_not(first))
+        def _():
+            @pl.loop(0, strip // GROUP)
+            def _(i):
+                planes = buf[:, group(i)].reshape(2 * nmode * GROUP, cols)
+                sums = jnp.dot(coef[...], planes, preferred_element_type=jnp.float32)
+                put(i, sums[:height] + sums[height:])
+
+        out_copy(j).start()
+
+    def within(j):
+        return jnp.logical_and(j >= 0, j < chunks)
+
+    @pl.loop(0, chunks + tree_lead)
+    def _(t):
+        @pl.when(t < chunks)
+        def _():
+            compute(t)
+            send_line((0, 1, 2), mode, t)
+
+            @pl.when(first)
+            def _():
+                send_tree(mode, t)
+
+        for d in range(1, nz):
+            for way, step in ((0, -d), (1, d)):
+                there = jnp.logical_and(z + step >= 0, z + step < nz)
+
+                @pl.when(jnp.logical_and(there, within(t - d)))
+                def _(way=way, step=step, d=d):
+                    slot = mode + step * LINE
+                    await_part(slot, t - d)
+                    send_line((way, 2), slot, t - d)
+
+                    @pl.when(first)
+                    def _():
+                        send_tree(slot, t - d)
+
+        @pl.when(within(t - own_lead))
+        def _():
+            for line in range(nz):
+                slot = line * LINE + 1 - x
+                await_part(slot, t - own_lead)
+
+                @pl.when(first)
+                def _():
+                    send_tree(slot, t - own_lead)
+
+        @pl.when(within(t - tree_lead))
+        def _():
+            @pl.when(jnp.logical_not(first))
+            def _():
+                for q in range(nmode):
+                    await_part(q + nmode, t - tree_lead)
+
+                    @pl.when(even)
+                    def _():
+                        tree_copy(0, q, t - tree_lead).start()
+
+            combine(t - tree_lead)
+
+    for j in range(max(chunks - 2, 0), chunks):
+        out_copy(j).wait()
+
+    @pl.loop(0, chunks)
+    def _(j):
+        for line in range(nz):
+            slot = line * LINE + x
+            for way, sent in ((0, z >= line), (1, z <= line), (2, z >= 0)):
+                @pl.when(jnp.logical_and(sent, peers[way][0]))
+                def _(way=way):
+                    line_copy(way, slot, j).wait_send()
+        for q in range(nmode):
+            for way in range(len(tree)):
+                @pl.when(tree[way][0])
+                def _(way=way):
+                    tree_copy(way, q, j).wait_send()
+
+
 def per_device_gather(control, filters, weights, vertical, balance):
     members, _, depth, rows, cols = control.shape
-    nmode = lax.axis_size("mode")
+    nmode, nvar = lax.axis_size("mode"), lax.axis_size("var")
     var = lax.axis_index("var")
-    filtered = smooth(control.reshape(members * depth, rows, cols), filters, weights[0])
-    first = lax.psum(jnp.where(var == 0, filtered, jnp.zeros_like(filtered)), "var")
-    both = jnp.stack([filtered, first]).reshape(2, members, depth, rows, cols)
-    both = lax.all_gather(both, "mode", axis=2, tiled=True)
     own, high, low = coefficients(vertical, balance, var, lax.axis_index("mode"), nmode)
-    coef = jnp.stack([own, high], axis=1)
-    levels = jnp.einsum("lsq,smqrc->mlrc", coef, both, preferred_element_type=jnp.float32)
-    levels += jnp.einsum("lq,mqrc->mlrc", low, both[1], preferred_element_type=jnp.float32)
-    return levels.astype(jnp.bfloat16)[:, None]
+    levels = own.shape[0]
+    coef = jnp.stack([jnp.stack([own, high], 1), jnp.stack([jnp.zeros_like(own), low], 1)])
+    coef = coef[:, :, None, :, :, None] * jnp.eye(GROUP, dtype=coef.dtype)[:, None, None, :]
+    coef = coef.reshape(2 * levels * GROUP, 2 * nmode * GROUP)
+    chunks = max(rows // 128, 1)
+    strip = rows // chunks
+    vmem = pl.BlockSpec(memory_space=pltpu.VMEM)
+    out = pl.pallas_call(
+        functools.partial(gather_kernel, nmode, nvar, chunks),
+        out_shape=jax.ShapeDtypeStruct((levels, rows, cols), jnp.bfloat16),
+        in_specs=[vmem] * 4,
+        out_specs=pl.BlockSpec(memory_space=pl.ANY),
+        scratch_shapes=[
+            pltpu.VMEM((2 * nmode, rows, cols), jnp.bfloat16),
+            pltpu.VMEM((2, levels, strip, cols), jnp.bfloat16),
+            pltpu.SemaphoreType.DMA((2 * nmode, chunks)),
+            pltpu.SemaphoreType.DMA((3, nmode // LINE, chunks)),
+            pltpu.SemaphoreType.DMA((max(nvar // 2, 1), nmode, chunks)),
+            pltpu.SemaphoreType.DMA((2,)),
+        ],
+        compiler_params=pltpu.CompilerParams(
+            collective_id=0, has_side_effects=True, vmem_limit_bytes=64 * 1000 * 1000
+        ),
+    )(control.reshape(rows, cols), filters, weights[0], coef)
+    return out.reshape(members, 1, levels, rows, cols)
 
 
 def solution(mesh):
     in_specs = (P(None, "var", "mode", None, None), P(), P("var", None, None, None), P(), P())
     out_specs = P(None, "var", "mode", None, None)
+    nmode, nvar = mesh.shape["mode"], mesh.shape["var"]
 
     def run(control, filters, weights, vertical, balance):
         members, _, modes, rows, cols = control.shape
-        gather = modes * mesh.shape["mode"] <= vertical.shape[1] * 2
+        planes = 2 * modes + 2 * filters.shape[0] + 1 + 2 * vertical.shape[1] // nmode // 8
+        gather = members == 1 and modes == nmode and nmode % LINE == 0 and nvar % 2 == 0
+        gather = gather and planes * rows * cols * 2 <= 56 * 2**20
         body = per_device_gather if gather else per_device_exchange
         return jax.shard_map(
             body, mesh=mesh, in_specs=in_specs, out_specs=out_specs, check_vma=False

time: 835 us -> 241 us (0.29)
  waiting for transfers between devices: 689 us -> 0 us
  Pallas kernels: 0 us -> 223 us
  matrix products: 88.9 us -> 0.81 us
  local copies, waits for them, and re-layouts: 35.1 us -> 16.4 us
  between operations: 13.4 us -> 0.04 us
    all_gather x1 -> x0, waiting for transfers between devices: 637 us -> none  [per_device_gather(): both = lax.all_gather(both, 'mode', axis=2, tiled=True)]
    pallas_call x0 -> x1, Pallas kernels: none -> 223 us  [per_device_gather(): pl.pallas_call(functools.partial(gather_kernel, nmode, nvar, chunks), out...]
    dot_general x5 -> x0, matrix products: 88.1 us -> none  [the longest x1 33.1 us: per_device_gather(): jnp.einsum('lsq,smqrc->mlrc', coef, both, preferred_element_type=jnp.floa...]
    psum x1 -> x0, waiting for transfers between devices: 52.1 us -> none  [per_device_gather(): lax.psum(jnp.where(var == 0, filtered, jnp.zeros_like(filtered)), 'var')]
    broadcast_in_dim x1 -> x0, local copies, waits for them, and re-layouts: 18.8 us -> none  [per_device_gather(): return levels.astype(jnp.bfloat16)[:, None]]
    another operation x1, local copies, waits for them, and re-layouts: 13.9 us -> 0.01 us  [per_device_gather(): jnp.stack([jnp.stack([own, high], 1), jnp.stack([jnp.zeros_like(own), low...]
    unnamed x9 -> x4, local copies, waits for them, and re-layouts: 2.34 us -> 14 us
  transfers between devices with their start and end apart: 2 -> 0, of which waited for: 2 -> 0; matrix products, arithmetic and copies ran while one was open for 0% -> 0% of each run, Pallas kernels for 0% -> 0%
where the time goes in v2:
time: 241 us
  Pallas kernels  223 us (93%)
  local copies, waits for them, and re-layouts  16.4 us (7%)
    pallas_call x1, Pallas kernels, per_device_gather(): pl.pallas_call(functools.partial(gather_kernel, nmode, nvar, chunks), out...  223 us
    unnamed x4, local copies, waits for them, and re-layouts  14 us

profile of v2, /device:TPU:29, one launch (start us, length us, event | category | flops | bytes accessed | tf_op | source)
XLA Modules:
  0.0 240.8 jit_solution(5031432864869255034)
XLA Ops:
  0.0 0.0 copy-start
  0.0 0.8 constant_dynamic-slice_fusion
  0.8 0.1 copy.8
  0.9 0.0 copy-done
  0.9 0.8 convert_bitcast_fusion
  1.7 0.1 broadcast_multiply_fusion
  1.9 1.7 mul.25.coef
  3.5 223.3 %shard_map.55 = bf16[8,1024,1024]{2,1,0:T(8,128)(2,1)} custom-call(bf16[1024,1024]{1,0:T(8,128)(2,1)} %bitcast.26, bf16[3,1024,1024]{2,1,0:T(8,128)(2,1)} %filters.1, bf16[3,1024,1024]{2,1,0:T(8,128)(2,1)} %bitcast.25, bf16[256,256]{1,0:T(8,128)(2,1)} %mul.25.coef), custom_call_target="tpu_custom_call" | custom-call | tf_op jit(solution)/shard_map/pallas_call | solution.py:279
  226.9 13.9 %copy.10 = bf16[1,1,8,1024,1024]{4,3,2,1,0:T(8,128)(2,1)} copy(bf16[1,1,8,1024,1024]{4,3,2,1,0:T(8,128)(2,1)} %bitcast.24) | data formatting | bytes 33554432
  (4 shorter events, 0.0 us)
Async XLA Ops:
  0.0 0.9 copy-start

commit v3 on v2

--- a/solution.py
+++ b/solution.py
@@ -75,24 +75,41 @@
 
 
 def gather_kernel(
-    nmode, nvar, chunks, control, filters, weights, coef, out,
-    buf, stage, recv, line_send, tree_send, out_sem,
+    nmode, nvar, chunks, control_in, filters_in, weights_in, coef, out,
+    buf, stage, control, filters, weights,
+    recv, line_send, tree_send, cross_send, out_sem, in_sem,
 ):
     mode, var = lax.axis_index("mode"), lax.axis_index("var")
     z, x = mode // LINE, mode % LINE
     nz = nmode // LINE
     rows, cols = control.shape
     strip = rows // chunks
-    own_lead = nz
-    tree_lead = nz + 2
-
+    short = chunks - chunks // 8
+    lead = 0
+    line_lag = lead + nz + 2
+    own_tree_lag = line_lag + 1
+    tree_lag = line_lag + 2
+
+    loads = [pltpu.make_async_copy(control_in, control, in_sem.at[0])]
+    loads += [
+        pltpu.make_async_copy(filters_in.at[k], filters.at[k], in_sem.at[2 * k + 1])
+        for k in range(filters.shape[0])
+    ]
+    fetches = [
+        pltpu.make_async_copy(weights_in.at[k], weights.at[k], in_sem.at[2 * k + 2])
+        for k in range(filters.shape[0])
+    ]
+    for load in loads + fetches:
+        load.start()
+
+    first = var == 0
     even = var % 2 == 0
+    later = jnp.logical_and(even, var > 0)
     peers = [
         (z < nz - 1, (mode + LINE, var)),
         (z > 0, (mode - LINE, var)),
         (var >= 0, (z * LINE + 1 - x, var)),
     ]
-    first = var == 0
     tree = [(even, (mode, var + 1))] + [
         (first, (mode, jnp.int32(v))) for v in range(2, nvar, 2)
     ]
@@ -101,7 +118,7 @@
     count = jnp.int32(0)
     greet = peers + tree + [
         (jnp.logical_not(even), (mode, var - 1)),
-        (jnp.logical_and(even, var > 0), (mode, jnp.int32(0))),
+        (later, (mode, jnp.int32(0))),
     ]
     for exists, device in greet:
         @pl.when(exists)
@@ -115,18 +132,22 @@
     def part(slot, j):
         return buf.at[slot, pl.ds(pl.multiple_of(j * strip, strip), strip)]
 
+    def remote(source, slot, j, send_sem, device):
+        return pltpu.make_async_remote_copy(
+            part(source, j), part(slot, j), send_sem, recv.at[slot, j],
+            device_id=device, device_id_type=pl.DeviceIdType.MESH,
+        )
+
     def line_copy(way, slot, j):
-        return pltpu.make_async_remote_copy(
-            part(slot, j), part(slot, j), line_send.at[way, slot // LINE, j], recv.at[slot, j],
-            device_id=peers[way][1], device_id_type=pl.DeviceIdType.MESH,
-        )
+        return remote(slot, slot, j, line_send.at[way, slot, j], peers[way][1])
 
     def tree_copy(way, q, j):
         source = jnp.where(first, q, q + nmode)
-        return pltpu.make_async_remote_copy(
-            part(source, j), part(q + nmode, j), tree_send.at[way, q, j], recv.at[q + nmode, j],
-            device_id=tree[way][1], device_id_type=pl.DeviceIdType.MESH,
-        )
+        return remote(source, q + nmode, j, tree_send.at[way, q, j], tree[way][1])
+
+    def cross_copy(line, j):
+        q = line * LINE + x
+        return remote(q + nmode, q + nmode, j, cross_send.at[line, j], peers[2][1])
 
     def await_part(slot, j):
         pltpu.make_async_copy(part(slot, j), part(slot, j), recv.at[slot, j]).wait()
@@ -137,21 +158,41 @@
             def _(way=way):
                 line_copy(way, slot, j).start()
 
-    def send_tree(q, j):
-        for way in range(len(tree)):
-            @pl.when(tree[way][0])
-            def _(way=way):
-                tree_copy(way, q, j).start()
-
-    def compute(j):
-        at = pl.ds(pl.multiple_of(j * strip, strip), strip)
-        total = jnp.zeros((strip, cols), jnp.float32)
+    def send_tree(own_line, q, j):
+        @pl.when(first)
+        def _():
+            tree_copy(0, q, j).start()
+            if own_line:
+                for way in range(1, len(tree)):
+                    tree_copy(way, q, j).start()
+            else:
+                @pl.when(j < short)
+                def _():
+                    for way in range(1, len(tree)):
+                        tree_copy(way, q, j).start()
+
+    depth = min(2 * strip, rows)
+
+    def compute(i):
+        at = pl.ds(pl.multiple_of(i * depth, depth), depth)
+        total = jnp.zeros((depth, cols), jnp.float32)
         for k in range(filters.shape[0]):
+            @pl.when(i == 0)
+            def _(k=k):
+                if k == 0:
+                    loads[0].wait()
+                loads[k + 1].wait()
+
             half = jnp.dot(filters[k, at], control[...], preferred_element_type=jnp.float32)
             full = lax.dot_general(
                 half.astype(jnp.bfloat16), filters[k], (((1,), (1,)), ((), ())),
                 preferred_element_type=jnp.float32,
             )
+
+            @pl.when(i == 0)
+            def _(k=k):
+                fetches[k].wait()
+
             total += weights[k, at].astype(jnp.float32) * full
         buf[mode, at] = total.astype(jnp.bfloat16)
 
@@ -198,53 +239,70 @@
     def within(j):
         return jnp.logical_and(j >= 0, j < chunks)
 
-    @pl.loop(0, chunks + tree_lead)
+    def arrivals(t):
+        for d in range(1, nz):
+            j = t - lead - d
+            for way, step in ((0, -d), (1, d)):
+                there = jnp.logical_and(z + step >= 0, z + step < nz)
+                there = jnp.logical_and(there, within(j))
+
+                @pl.when(there)
+                def _(way=way, step=step, j=j):
+                    slot = mode + step * LINE
+                    await_part(slot, j)
+                    send_line((way, 2), slot, j)
+                    send_tree(True, slot, j)
+
+    @pl.loop(0, chunks + tree_lag)
     def _(t):
         @pl.when(t < chunks)
         def _():
-            compute(t)
-            send_line((0, 1, 2), mode, t)
-
-            @pl.when(first)
-            def _():
-                send_tree(mode, t)
-
-        for d in range(1, nz):
-            for way, step in ((0, -d), (1, d)):
-                there = jnp.logical_and(z + step >= 0, z + step < nz)
-
-                @pl.when(jnp.logical_and(there, within(t - d)))
-                def _(way=way, step=step, d=d):
-                    slot = mode + step * LINE
-                    await_part(slot, t - d)
-                    send_line((way, 2), slot, t - d)
-
-                    @pl.when(first)
-                    def _():
-                        send_tree(slot, t - d)
-
-        @pl.when(within(t - own_lead))
+            @pl.when(t % (depth // strip) == 0)
+            def _():
+                compute(t // (depth // strip))
+
+            send_line((2, 0, 1), mode, t)
+            send_tree(True, mode, t)
+
+        arrivals(t)
+
+        @pl.when(within(t - line_lag))
         def _():
             for line in range(nz):
                 slot = line * LINE + 1 - x
-                await_part(slot, t - own_lead)
-
-                @pl.when(first)
+                await_part(slot, t - line_lag)
+                send_tree(False, slot, t - line_lag)
+
+        @pl.when(jnp.logical_and(later, within(t - own_tree_lag)))
+        def _():
+            j = t - own_tree_lag
+            for line in range(nz):
+                q = line * LINE + x
+                await_part(q + nmode, j)
+
+                @pl.when(j >= short)
                 def _():
-                    send_tree(slot, t - own_lead)
-
-        @pl.when(within(t - tree_lead))
-        def _():
-            @pl.when(jnp.logical_not(first))
+                    cross_copy(line, j).start()
+
+                tree_copy(0, q, j).start()
+
+        @pl.when(within(t - tree_lag))
+        def _():
+            j = t - tree_lag
+
+            @pl.when(later)
+            def _():
+                for line in range(nz):
+                    q = line * LINE + 1 - x
+                    await_part(q + nmode, j)
+                    tree_copy(0, q, j).start()
+
+            @pl.when(jnp.logical_not(even))
             def _():
                 for q in range(nmode):
-                    await_part(q + nmode, t - tree_lead)
-
-                    @pl.when(even)
-                    def _():
-                        tree_copy(0, q, t - tree_lead).start()
-
-            combine(t - tree_lead)
+                    await_part(q + nmode, j)
+
+            combine(j)
 
     for j in range(max(chunks - 2, 0), chunks):
         out_copy(j).wait()
@@ -252,16 +310,32 @@
     @pl.loop(0, chunks)
     def _(j):
         for line in range(nz):
-            slot = line * LINE + x
-            for way, sent in ((0, z >= line), (1, z <= line), (2, z >= 0)):
+            mine, other = line * LINE + x, line * LINE + 1 - x
+            for way, sent in ((0, z >= line), (1, z <= line)):
                 @pl.when(jnp.logical_and(sent, peers[way][0]))
                 def _(way=way):
-                    line_copy(way, slot, j).wait_send()
-        for q in range(nmode):
-            for way in range(len(tree)):
-                @pl.when(tree[way][0])
-                def _(way=way):
-                    tree_copy(way, q, j).wait_send()
+                    line_copy(way, mine, j).wait_send()
+
+            line_copy(2, mine, j).wait_send()
+
+            @pl.when(jnp.logical_and(later, j >= short))
+            def _():
+                cross_copy(line, j).wait_send()
+
+            @pl.when(even)
+            def _():
+                tree_copy(0, mine, j).wait_send()
+                tree_copy(0, other, j).wait_send()
+
+            @pl.when(first)
+            def _():
+                for way in range(1, len(tree)):
+                    tree_copy(way, mine, j).wait_send()
+
+                @pl.when(j < short)
+                def _():
+                    for way in range(1, len(tree)):
+                        tree_copy(way, other, j).wait_send()
 
 
 def per_device_gather(control, filters, weights, vertical, balance):
@@ -273,21 +347,26 @@
     coef = jnp.stack([jnp.stack([own, high], 1), jnp.stack([jnp.zeros_like(own), low], 1)])
     coef = coef[:, :, None, :, :, None] * jnp.eye(GROUP, dtype=coef.dtype)[:, None, None, :]
     coef = coef.reshape(2 * levels * GROUP, 2 * nmode * GROUP)
-    chunks = max(rows // 128, 1)
+    chunks = max(rows // 64, 1)
     strip = rows // chunks
     vmem = pl.BlockSpec(memory_space=pltpu.VMEM)
     out = pl.pallas_call(
         functools.partial(gather_kernel, nmode, nvar, chunks),
         out_shape=jax.ShapeDtypeStruct((levels, rows, cols), jnp.bfloat16),
-        in_specs=[vmem] * 4,
+        in_specs=[pl.BlockSpec(memory_space=pl.ANY)] * 3 + [vmem],
         out_specs=pl.BlockSpec(memory_space=pl.ANY),
         scratch_shapes=[
             pltpu.VMEM((2 * nmode, rows, cols), jnp.bfloat16),
             pltpu.VMEM((2, levels, strip, cols), jnp.bfloat16),
+            pltpu.VMEM((rows, cols), jnp.bfloat16),
+            pltpu.VMEM(filters.shape, jnp.bfloat16),
+            pltpu.VMEM(filters.shape, jnp.bfloat16),
             pltpu.SemaphoreType.DMA((2 * nmode, chunks)),
-            pltpu.SemaphoreType.DMA((3, nmode // LINE, chunks)),
-            pltpu.SemaphoreType.DMA((max(nvar // 2, 1), nmode, chunks)),
+            pltpu.SemaphoreType.DMA((3, nmode, chunks)),
+            pltpu.SemaphoreType.DMA((nvar // 2, nmode, chunks)),
+            pltpu.SemaphoreType.DMA((nmode // LINE, chunks)),
             pltpu.SemaphoreType.DMA((2,)),
+            pltpu.SemaphoreType.DMA((2 * filters.shape[0] + 1,)),
         ],
         compiler_params=pltpu.CompilerParams(
             collective_id=0, has_side_effects=True, vmem_limit_bytes=64 * 1000 * 1000

time: 241 us -> 236 us (0.979)
  Pallas kernels: 223 us -> 217 us
    pallas_call x1, Pallas kernels: 223 us -> 217 us  [per_device_gather(): pl.pallas_call(functools.partial(gather_kernel, nmode, nvar, chunks), out...]
where the time goes in v3:
time: 236 us; the launch traced here: 235 us
  Pallas kernels  217 us (92%)
  local copies, waits for them, and re-layouts  16.4 us (7%)
    pallas_call x1, Pallas kernels, per_device_gather(): pl.pallas_call(functools.partial(gather_kernel, nmode, nvar, chunks), out...  217 us
    unnamed x4, local copies, waits for them, and re-layouts  14 us

profile of v3, /device:TPU:29, one launch (start us, length us, event | category | flops | bytes accessed | tf_op | source)
XLA Modules:
  0.0 234.7 jit_solution(12976429556017949538)
XLA Ops:
  0.0 0.0 copy-start
  0.0 0.8 constant_dynamic-slice_fusion
  0.8 0.1 copy.8
  0.9 0.0 copy-done
  0.9 0.8 convert_bitcast_fusion
  1.7 0.1 broadcast_multiply_fusion
  1.9 1.7 mul.25.coef
  3.5 217.2 %shard_map.55 = bf16[8,1024,1024]{2,1,0:T(8,128)(2,1)} custom-call(bf16[1024,1024]{1,0:T(8,128)(2,1)} %bitcast.26, bf16[3,1024,1024]{2,1,0:T(8,128)(2,1)} %filters_in.1, bf16[3,1024,1024]{2,1,0:T(8,128)(2,1)} %bitcast.25, bf16[256,256]{1,0:T(8,128)(2,1)} %mul.25.coef), custom_call_target="tpu_custom_call" | custom-call | tf_op jit(solution)/shard_map/pallas_call | solution.py:353
  220.8 13.9 %copy.10 = bf16[1,1,8,1024,1024]{4,3,2,1,0:T(8,128)(2,1)} copy(bf16[1,1,8,1024,1024]{4,3,2,1,0:T(8,128)(2,1)} %bitcast.24) | data formatting | bytes 33554432
  (4 shorter events, 0.0 us)
Async XLA Ops:
  0.0 0.9 copy-start
